TPU v7x, 32 devices: a whole 2x2x4 slice. The times are simulated.
32 devices in a mesh: grp: 2 (over z_hi), seq: 8 (over y, x, core), tp: 2 (over z_lo).
Axes of the slice: x: 2, y: 2, z: 4 (z_hi: 2, z_lo: 2; z = z_hi * 2 + z_lo), core: 2. Of those that a mesh axis runs over, the one named last changes fastest.
Arguments:
- latents: bfloat16 [2, 64, 2048], P('grp', None, 'seq'), may hold values from -6 to 6
- patch_weight: bfloat16 [128, 5120], replicated, may hold values from -0.5 to 0.5
- patch_bias: float32 [5120], replicated, may hold values from -3 to 3
- modulation: float32 [3, 5120], replicated, may hold values from -3 to 3
- qkv_weight: bfloat16 [5120, 3, 1024], P(None, None, 'seq'), may hold values from -0.078125 to 0.078125
- norm_gain: float32 [2, 1024], P(None, 'seq'), may hold values from 0.5 to 16
- out_weight: bfloat16 [1024, 5120], P('seq', ('grp', 'tp')), may hold values from -0.5 to 0.5
- token_order: int32 [2048], replicated, may hold values from 0 to 2047, each once
- window_start: int32 [1], replicated, may hold values from 0 to 1024
Outputs:
- attended: bfloat16 [1024, 5120], P('seq', ('grp', 'tp'))
Inputs may be any that keep to these rules, and one draw needn't show every extreme that they name: Position j of the target layout holds frame-major token token_order[j]; every token stands once. The window covers target positions window_start[0] to window_start[0] + 1023.
All inputs are finite; a program needn't handle non-finite values.
Results may differ from a plain program's by a relative error of at most 0.018.
The roundings to bfloat16 on the way count: a program that leaves them out, or rounds other values in their place, can miss the bound.
Values may be sent and summed in bfloat16 or wider, within the bound.
A program may use at most 128 MiB of HBM per device.

v0:
```python
import math
import jax
import jax.numpy as jnp
from jax import lax
from jax.sharding import PartitionSpec as P

QW_DEV = 128
norm_eps = 0.1


def swapped(block, axis, apart):
    count = lax.axis_size(axis)
    route = []
    for low in range(count):
        high = low | 1 << apart
        if high != low and high < count:
            route += [(low, high), (high, low)]
    return lax.ppermute(block, axis, route)


def joined(array, axis, combine):
    everything = jax.tree.map(lambda part: lax.all_gather(part, axis), array)
    initial = jax.tree.map(lambda part: part[0], everything)

    def step(k, so_far):
        return combine(so_far, jax.tree.map(lambda part: part[k], everything))

    return lax.fori_loop(1, lax.axis_size(axis), step, initial)


def embed_rows(columns, patch_weight, patch_bias, modulation):
    channels = columns.shape[1]
    weight = patch_weight.reshape(2, channels, patch_weight.shape[1])
    embedded = (
        lax.dot_general(
            columns, weight, (((0, 1), (0, 1)), ((), ())), preferred_element_type=jnp.float32
        )
        + patch_bias
    )
    centre = embedded - jnp.mean(embedded, axis=1, keepdims=True)
    spread = jnp.mean(centre * centre, axis=1, keepdims=True)
    normed = centre * lax.rsqrt(spread + norm_eps) * (1.0 + modulation[1]) + modulation[0]
    return normed.astype(jnp.bfloat16)


def project_rows(columns, flat_weight, patch_weight, patch_bias, modulation):
    row_total = columns.shape[2]
    block = math.gcd(row_total, 512)

    def one_block(block_index):
        section = lax.dynamic_slice_in_dim(columns, block_index * block, block, 2)
        normed = embed_rows(section, patch_weight, patch_bias, modulation)
        return jnp.dot(normed, flat_weight, preferred_element_type=jnp.float32)

    result = lax.map(one_block, jnp.arange(row_total // block))
    return result.reshape(row_total, flat_weight.shape[1])


def per_device(
    latents,
    patch_weight,
    patch_bias,
    modulation,
    qkv_weight,
    norm_gain,
    out_weight,
    token_order,
    window_start,
):
    head_dim = qkv_weight.shape[2]
    seq_count = lax.axis_size("seq")
    groups = lax.axis_size("grp") * lax.axis_size("tp")
    quarter = lax.axis_index("grp") * lax.axis_size("tp") + lax.axis_index("tp")
    partner = swapped(latents, "grp", 0)
    is_high = lax.axis_index("grp") == 0
    paired = jnp.where(
        is_high, jnp.concatenate([latents, partner], 0), jnp.concatenate([partner, latents], 0)
    )
    gathered = lax.all_gather(paired, "seq", axis=2, tiled=True)
    tokens = gathered.shape[2]
    key_count = tokens // groups
    flat_weight = qkv_weight.reshape(qkv_weight.shape[0], 3 * head_dim)
    key_columns = lax.dynamic_slice_in_dim(gathered, quarter * key_count, key_count, 2)
    pair_raw = project_rows(
        key_columns, flat_weight[:, head_dim:], patch_weight, patch_bias, modulation
    )
    key_raw = pair_raw[:, :head_dim]
    values = pair_raw[:, head_dim:].astype(jnp.bfloat16)
    window_len = QW_DEV * seq_count
    window_rows = lax.dynamic_slice_in_dim(token_order, window_start[0], window_len)
    part_len = window_len // groups
    query_rows = lax.dynamic_slice_in_dim(window_rows, quarter * part_len, part_len)
    query_columns = jnp.take(gathered, query_rows, axis=2)
    query_raw = project_rows(
        query_columns, flat_weight[:, :head_dim], patch_weight, patch_bias, modulation
    )
    query_total, key_total = lax.psum(
        (jnp.sum(query_raw * query_raw, axis=1), jnp.sum(key_raw * key_raw, axis=1)), "seq"
    )
    norm_width = head_dim * seq_count
    queries = (
        query_raw * lax.rsqrt(query_total[:, None] / norm_width + norm_eps) * norm_gain[0]
    ).astype(jnp.bfloat16)
    key_rows = (
        key_raw * lax.rsqrt(key_total[:, None] / norm_width + norm_eps) * norm_gain[1]
    ).astype(jnp.bfloat16)
    queries = lax.all_gather(queries, ("grp", "tp"), axis=0, tiled=True)
    query_len = queries.shape[0]
    query_block = math.gcd(query_len, 512)
    score_scale = head_dim ** (-0.5)

    def attend(block_index):
        query_part = lax.dynamic_slice_in_dim(queries, block_index * query_block, query_block, 0)
        scores = (
            lax.dot_general(
                query_part, key_rows, (((1,), (1,)), ((), ())), preferred_element_type=jnp.float32
            )
            * score_scale
        )
        row_max = jnp.max(scores, axis=1)
        probs = jnp.exp(scores - row_max[:, None])
        row_sum = jnp.sum(probs, axis=1)
        row_acc = jnp.dot(probs.astype(jnp.bfloat16), values, preferred_element_type=jnp.float32)
        return (row_max, row_sum, row_acc)

    maxima, sums, accums = lax.map(attend, jnp.arange(query_len // query_block))
    maxima = maxima.reshape(query_len)
    sums = sums.reshape(query_len)
    accums = accums.reshape(query_len, head_dim)

    def combine(first, second):
        row_max = jnp.maximum(first[0], second[0])
        first_factor = jnp.exp(first[0] - row_max)
        second_factor = jnp.exp(second[0] - row_max)
        row_sum = first[1] * first_factor + second[1] * second_factor
        row_acc = first[2] * first_factor[:, None] + second[2] * second_factor[:, None]
        return (row_max, row_sum, row_acc)

    row_max, row_sum, row_acc = joined((maxima, sums, accums), ("grp", "tp"), combine)
    attention = (row_acc / row_sum[:, None]).astype(jnp.bfloat16)
    cols_dev = out_weight.shape[1]
    gate_cols = lax.dynamic_slice_in_dim(modulation[2], quarter * cols_dev, cols_dev)
    regrouped = lax.all_to_all(attention, "seq", split_axis=0, concat_axis=1, tiled=True)
    mixed_out = jnp.dot(
        regrouped,
        lax.all_gather(out_weight, "seq", axis=0, tiled=True),
        preferred_element_type=jnp.float32,
    )
    return (mixed_out * gate_cols).astype(jnp.bfloat16)


def solution(mesh):
    in_specs = (
        P("grp", None, "seq"),
        P(),
        P(),
        P(),
        P(None, None, "seq"),
        P(None, "seq"),
        P("seq", ("grp", "tp")),
        P(),
        P(),
    )
    out_specs = P("seq", ("grp", "tp"))
    return jax.shard_map(
        per_device, mesh=mesh, in_specs=in_specs, out_specs=out_specs, check_vma=False
    )
```

profile of v0, /device:TPU:0, one launch (start us, length us, event | category | flops | bytes accessed | tf_op | source)
XLA Modules:
  0.0 168.9 jit_solution(8679716140680726561)
XLA Ops:
  6.5 4.1 %collective-permute-start = (bf16[1,64,256]{2,1,0:T(8,128)(2,1)}, bf16[1,64,256]{2,1,0:T(8,128)(2,1)S(1)}, u32[]{:S(2)}, u32[]{:S(2)}) collective-permute-start(bf16[1,64,256]{2,1,0:T(8,128)(2,1)} %param.13), channel_id=1, source_target_pairs={{0,16},{16,0},{1,17},{17,1},{2,18},{18,2},{3,19},{19,3},{4,20},{20... | collective-permute-start | bytes 98312 | tf_op jit(solution)/shard_map/ppermute | solution.py:18
  11.3 1.7 %fusion.22 = (f32[1,5120]{1,0:T(1,128)}, f32[1,5120]{1,0:T(1,128)S(1)}, f32[1,5120]{1,0:T(1,128)S(1)}) fusion(f32[3,5120]{1,0:T(4,128)} %param.16), kind=kLoop, calls=%fused_computation.62 | loop fusion | flops 5120 | bytes 122880 | tf_op jit(solution)/shard_map/slice | solution.py:142
  15.7 6.3 %copy.28 = bf16[5120,3,128]{0,2,1:T(8,128)(2,1)} copy(bf16[5120,3,128]{2,0,1:T(8,128)(2,1)} %param.17) | data formatting | bytes 7864320 | tf_op args[4]
  22.0 10.9 %all_gather.18 = bf16[2,64,2048]{2,1,0:T(8,128)(2,1)S(1)} all-gather(bf16[2,64,256]{2,1,0:T(8,128)(2,1)S(1)} %maximum_select_fusion), channel_id=1, replica_groups=mesh['grp'=2,'seq'=8,'tp'=2] {'seq'}, dimensions={2}, use_global_device_ids=true | all-gather | bytes 589824 | tf_op jit(solution)/shard_map/all_gather | solution.py:79
  33.7 1.6 fusion.9
  35.4 1.6 multiply_reduce_fusion
  37.5 2.5 %fusion.11 = f32[512,256]{0,1:T(8,128)S(1)} fusion(f32[512,5120,1]{1,0,2:T(8,128)S(1)} %get-tuple-element.357, f32[5120]{0:T(1024)S(1)} %bitcast.97, f32[5120]{0:T(1024)S(1)} %bitcast.95, f32[512]{0:T(512)S(1)} %add_rsqrt_fusion.1, f32[512]{0:T(512)S(1)} %broadcast_multiply_fusion, f32[5120]{0:T(1024)S(1)} %copy-done.3, bf16[5120,384]{0,1:T(8,128)(2,1)S(1)} %bitcast.83), kind=kOutput, calls=%fused_computation.26 | convolution fusion | flops 1357905920 | bytes 13697024 | tf_op jit(solution)/shard_map/while/body/eval_jaxpr/dot_general | solution.py:53
  40.1 1.6 gather_fusion
  42.9 1.7 %fusion.23 = (f32[256]{0:T(256)S(1)}, f32[256,5120]{1,0:T(8,128)S(1)}) fusion(f32[5120]{0:T(1024)} %param.15, bf16[2,64,5120]{2,1,0:T(8,128)(2,1)S(1)} %bitcast.80, bf16[2,64,256]{1,0,2:T(2,128)(2,1)S(1)} %fusion.19), kind=kOutput, calls=%fused_computation.63 | convolution fusion | flops 338165504 | bytes 6640640 | tf_op jit(solution)/shard_map/while/body/eval_jaxpr/dot_general | solution.py:35
  45.4 2.6 %multiply_reduce_fusion.3 = (f32[256]{0:T(256)S(1)}, f32[256,128]{0,1:T(8,128)S(1)}) fusion(bf16[5120,384]{0,1:T(8,128)(2,1)} %bitcast.82, f32[256,5120]{1,0:T(8,128)S(1)} %get-tuple-element.353, f32[5120]{0:T(1024)S(1)} %bitcast.98, f32[5120]{0:T(1024)S(1)} %bitcast.96, f32[256]{0:T(256)S(1)} %add_rsqrt_fusion.3, f32[256]{0:T(256)S(1)} %broadcast_multiply_fusion.1), kind=kOutput, calls=%fused_computation.42 | convolution fusion | flops 342163200 | bytes 6728704 | tf_op jit(solution)/shard_map/while/body/eval_jaxpr/dot_general | solution.py:53
  47.9 13.2 %all-reduce = (f32[256]{0:T(256)S(1)}, f32[512]{0:T(512)S(1)}) all-reduce(f32[256]{0:T(256)S(1)} %get-tuple-element.354, f32[512]{0:T(512)S(1)} %multiply_reduce_fusion.2), channel_id=1, replica_groups=mesh['grp'=2,'seq'=8,'tp'=2] {'seq'}, use_global_device_ids=true, to_apply=%region_3.4 | all-reduce | flops 768 | bytes 6144 | tf_op jit(solution)/shard_map/psum | solution.py:97
  61.5 14.4 %all_gather.19 = bf16[1024,128]{0,1:T(8,128)(2,1)S(1)} all-gather(bf16[256,128]{0,1:T(8,128)(2,1)S(1)} %multiply_convert_fusion.1), channel_id=1, replica_groups=mesh['grp'=2,'seq'=8,'tp'=2] {'grp','tp'}, dimensions={0}, use_global_device_ids=true | all-gather | bytes 327680 | tf_op jit(solution)/shard_map/all_gather | solution.py:107
  76.0 4.4 %while.11 = (s32[]{:T(128)}, f32[2,512]{1,0:T(2,128)S(1)}, f32[2,512]{1,0:T(2,128)S(1)}, f32[2,512,128]{2,1,0:T(8,128)S(1)}, s32[2]{0:T(128)S(1)}, /*index=5*/bf...) while((s32[]{:T(128)}, f32[2,512]{1,0:T(2,128)S(1)}, ...), condition=%wide.region_11.12_spmd, body=%wide.region_8.11_spmd.sunk | while | flops 135789568 | bytes 3817663 | solution.py:126
  82.0 13.5 %all-gather = f32[4,1,1024]{2,1,0:T(1,128)S(1)} all-gather(f32[1,1,1024]{2,1,0:T(1,128)S(1)} %reshape.73), channel_id=1, replica_groups=mesh['grp'=2,'seq'=8,'tp'=2] {'grp','tp'}, dimensions={0}, use_global_device_ids=true | all-gather | bytes 20480 | tf_op jit(solution)/shard_map/all_gather | solution.py:22
  95.6 13.8 %all-gather.1 = f32[4,1,1024]{2,1,0:T(1,128)S(1)} all-gather(f32[1,1,1024]{2,1,0:T(1,128)S(1)} %reshape.75), channel_id=1, replica_groups=mesh['grp'=2,'seq'=8,'tp'=2] {'grp','tp'}, dimensions={0}, use_global_device_ids=true | all-gather | bytes 20480 | tf_op jit(solution)/shard_map/all_gather | solution.py:22
  109.4 16.2 %all-gather.5.cloned.1.call-done = f32[4,1024,128]{2,1,0:T(8,128)} async-done(((f32[1,1024,128]{2,1,0:T(8,128)}), f32[4,1024,128]{2,1,0:T(8,128)}) %all-gather.5.cloned.1.call-update) | async-done | bytes 2097168 | tf_op jit(solution)/shard_map/all_gather | solution.py:22
  126.7 4.7 %while.42 = (s32[]{:T(128)}, f32[1024]{0:T(1024)S(1)}, f32[1024]{0:T(1024)S(1)}, f32[1024,128]{1,0:T(8,128)S(1)}, f32[4,1024]{1,0:T(4,128)S(1)}, /*index=5*/f32[...) while((s32[]{:T(128)}, f32[1024]{0:T(1024)S(1)}, f32[1024]{0:T(1024)S(1)}, ...), condition=%wide.region_13.14_spmd, body=%wide.region_12.13_spmd.sunk | while | flops 399365 | bytes 1630359 | solution.py:28
  126.8 1.5 fusion.43
  128.3 1.5 fusion.43
  129.9 1.5 fusion.43
  132.3 3.6 %all-to-all-start = ((bf16[8,128,128]{2,1,0:T(8,128)(2,1)}), bf16[8,128,128]{2,1,0:T(8,128)(2,1)S(1)}, u32[]{:S(2)}, u32[]{:S(2)}) async-start(bf16[8,128,128]{2,1,0:T(8,128)(2,1)} %bitcast.21), calls=%async_computation | async-start | bytes 524288 | tf_op jit(solution)/shard_map/all_to_all | solution.py:143
  136.6 7.0 %all-to-all-done = bf16[8,128,128]{2,1,0:T(8,128)(2,1)S(1)} async-done(((bf16[8,128,128]{2,1,0:T(8,128)(2,1)}), bf16[8,128,128]{2,1,0:T(8,128)(2,1)S(1)}, u32[]{:S(2)}, u32[]{:S(2)}) %all-to-all-start) | async-done | bytes 262176 | tf_op jit(solution)/shard_map/all_to_all | solution.py:143
  143.8 15.3 %all-gather.7.cloned.1.call-done = bf16[1024,1280]{1,0:T(8,128)(2,1)} async-done(((bf16[128,1280]{1,0:T(8,128)(2,1)}), bf16[1024,1280]{1,0:T(8,128)(2,1)}) %all-gather.7.cloned.1.call-update) | async-done | bytes 2621456 | tf_op jit(solution)/shard_map/all_gather | solution.py:146
  159.1 3.0 %fusion.14 = bf16[128,1280]{1,0:T(8,128)(2,1)} fusion(bf16[128,1024]{0,1:T(8,128)(2,1)S(1)} %bitcast.84, bf16[1024,1280]{1,0:T(8,128)(2,1)} %all-gather.7.cloned.1.call-done, f32[1280]{0:T(1024)S(1)} %dynamic-slice_reduce_fusion), kind=kOutput, calls=%fused_computation.30 | convolution fusion | flops 335872000 | bytes 3216384 | tf_op jit(solution)/shard_map/dot_general | solution.py:144
  (78 shorter events, 13.9 us)
Async XLA Ops:
  6.5 27.2 %copy-start = (bf16[128,5120]{1,0:T(8,128)(2,1)S(1)}, bf16[128,5120]{1,0:T(8,128)(2,1)}, u32[]{:S(2)}) copy-start(bf16[128,5120]{1,0:T(8,128)(2,1)} %param.14) | copy-start | bytes 3932164
  6.5 15.5 %copy-start.4 = (bf16[1,64,256]{2,1,0:T(8,128)(2,1)S(1)}, bf16[1,64,256]{2,1,0:T(8,128)(2,1)}, u32[]{:S(2)}) copy-start(bf16[1,64,256]{2,1,0:T(8,128)(2,1)} %param.13) | copy-start | bytes 98308
  6.5 27.2 %copy-start.3 = (f32[5120]{0:T(1024)S(1)}, f32[5120]{0:T(1024)}, u32[]{:S(2)}) copy-start(f32[5120]{0:T(1024)} %param.15) | copy-start | bytes 61444
  6.5 119.1 %all-gather.5.cloned.1.call-start = ((), (), s32[]{:S(2)}) async-start(), calls=%async_computation.1 | async-start | bytes 2621440 | tf_op jit(solution)/shard_map/all_gather | solution.py:22
  6.5 15.5 %collective-permute-start = (bf16[1,64,256]{2,1,0:T(8,128)(2,1)}, bf16[1,64,256]{2,1,0:T(8,128)(2,1)S(1)}, u32[]{:S(2)}, u32[]{:S(2)}) collective-permute-start(bf16[1,64,256]{2,1,0:T(8,128)(2,1)} %param.13), channel_id=1, source_target_pairs={{0,16},{16,0},{1,17},{17,1},{2,18},{18,2},{3,19},{19,3},{4,20},{20... | collective-permute-start | bytes 98312 | tf_op jit(solution)/shard_map/ppermute | solution.py:18
  13.0 23.9 %copy-start.5 = (f32[1,5120]{1,0:T(1,128)}, f32[1,5120]{1,0:T(1,128)S(1)}, u32[]{:S(2)}) copy-start(f32[1,5120]{1,0:T(1,128)S(1)} %get-tuple-element.348) | copy-start | bytes 61444
  13.0 24.0 %copy-start.7 = (f32[1,5120]{1,0:T(1,128)}, f32[1,5120]{1,0:T(1,128)S(1)}, u32[]{:S(2)}) copy-start(f32[1,5120]{1,0:T(1,128)S(1)} %get-tuple-element.349) | copy-start | bytes 61444
  35.4 2.1 %copy-start.1 = (bf16[5120,3,128]{0,2,1:T(8,128)(2,1)S(1)}, bf16[5120,3,128]{0,2,1:T(8,128)(2,1)}, u32[]{:S(2)}) copy-start(bf16[5120,3,128]{0,2,1:T(8,128)(2,1)} %copy.28) | copy-start | bytes 11796484
  42.9 2.4 %copy-start.6 = (f32[1,5120]{1,0:T(1,128)S(1)}, f32[1,5120]{1,0:T(1,128)}, u32[]{:S(2)}) copy-start(f32[1,5120]{1,0:T(1,128)} %copy-done.5) | copy-start | bytes 61444
  42.9 2.4 %copy-start.8 = (f32[1,5120]{1,0:T(1,128)S(1)}, f32[1,5120]{1,0:T(1,128)}, u32[]{:S(2)}) copy-start(f32[1,5120]{1,0:T(1,128)} %copy-done.7) | copy-start | bytes 61444
  45.3 15.8 %copy-start.10 = (f32[128]{0:T(128)S(1)}, f32[128]{0:T(128)}, u32[]{:S(2)}) copy-start(f32[128]{0:T(128)} %get-tuple-element.350) | copy-start | bytes 1540
  45.3 16.0 %copy-start.9 = (f32[128]{0:T(128)S(1)}, f32[128]{0:T(128)}, u32[]{:S(2)}) copy-start(f32[128]{0:T(128)} %get-tuple-element.351) | copy-start | bytes 1540
  80.4 0.8 copy-start.2
  81.3 77.8 %all-gather.7.cloned.1.call-start = ((), (), s32[]{:S(2)}) async-start(), calls=%async_computation.2 | async-start | bytes 2949120 | tf_op jit(solution)/shard_map/all_gather | solution.py:146
  132.3 11.3 %all-to-all-start = ((bf16[8,128,128]{2,1,0:T(8,128)(2,1)}), bf16[8,128,128]{2,1,0:T(8,128)(2,1)S(1)}, u32[]{:S(2)}, u32[]{:S(2)}) async-start(bf16[8,128,128]{2,1,0:T(8,128)(2,1)} %bitcast.21), calls=%async_computation | async-start | bytes 524288 | tf_op jit(solution)/shard_map/all_to_all | solution.py:143
Sparse Core Ops, SparseCore 0:
  81.4 44.2 all-gather.4
  127.5 31.5 all-gather.6
where the time goes:
time: 170 us; the launch traced here: 169 us
  blocking collectives  65.9 us (39%)
  waiting for transfers between devices  39.2 us (23%)
  local copies, waits for them, and re-layouts  15 us (9%)
  between operations  14.3 us (8%)
  matrix products  12.8 us (8%)
  other arithmetic  12.6 us (7%)
  starting transfers between devices  7.78 us (5%)
    all_gather x2, blocking collectives, joined(): everything = jax.tree.map(lambda part: lax.all_gather(part, axis), array)  27.3 us
    all_gather x1, waiting for transfers between devices, joined(): everything = jax.tree.map(lambda part: lax.all_gather(part, axis), array)  16.2 us
    all_gather x1, waiting for transfers between devices, per_device(): lax.all_gather(out_weight, 'seq', axis=0, tiled=True)  15.3 us
    all_gather x1, blocking collectives, per_device(): queries = lax.all_gather(queries, ('grp', 'tp'), axis=0, tiled=True)  14.4 us
    psum x1, blocking collectives, per_device(): lax.psum((jnp.sum(query_raw * query_raw, axis=1), jnp.sum(key_raw * key_r...  13.2 us
    all_gather x1, blocking collectives, per_device(): gathered = lax.all_gather(paired, 'seq', axis=2, tiled=True)  10.9 us
    unnamed x27, local copies, waits for them, and re-layouts  7.73 us
    all_to_all x1, waiting for transfers between devices, per_device(): lax.all_to_all(attention, 'seq', split_axis=0, concat_axis=1, tiled=True)  6.96 us
  transfers between devices with their start and end apart: 4, of which 3 were waited for; matrix products, arithmetic and copies ran while one was open for 11% of the time, Pallas kernels for 0%

commit v1 on v0

--- a/solution.py
+++ b/solution.py
@@ -1,3 +1,4 @@
+import functools
 import math
 import jax
 import jax.numpy as jnp
@@ -6,6 +7,23 @@
 
 QW_DEV = 128
 norm_eps = 0.1
+
+
+def close_the_plane(inner_x, array_axis):
+    k_all = jax.lax.axis_size("seq")
+    leaves = [(idx, (idx + 1) % k_all) for idx in range(k_all)]
+    item_now = [None] * k_all
+    item_now[k_all - 1] = inner_x
+    for dev in range(k_all - 2, -1, -1):
+        item_now[dev] = jax.lax.ppermute(item_now[dev + 1], "seq", leaves)
+    r1 = jnp.concatenate(item_now, axis=array_axis)
+    s_next = jax.lax.axis_index("seq")
+    f_next = (s_next + 1) * inner_x.shape[array_axis]
+    m_next = jnp.roll(r1, f_next, array_axis)
+    return m_next
+
+
+cells_name = functools.partial(close_the_plane, array_axis=2)
 
 
 def swapped(block, axis, apart):
@@ -76,7 +94,7 @@
     paired = jnp.where(
         is_high, jnp.concatenate([latents, partner], 0), jnp.concatenate([partner, latents], 0)
     )
-    gathered = lax.all_gather(paired, "seq", axis=2, tiled=True)
+    gathered = cells_name(paired)
     tokens = gathered.shape[2]
     key_count = tokens // groups
     flat_weight = qkv_weight.reshape(qkv_weight.shape[0], 3 * head_dim)

time: 170 us -> 188 us (1.11)
  waiting for transfers between devices: 39.2 us -> 68.6 us
  blocking collectives: 65.9 us -> 53.7 us
    ppermute x0 -> x7, waiting for transfers between devices: none -> 24.5 us  [close_the_plane(): item_now[dev] = jax.lax.ppermute(item_now[dev + 1], 'seq', leaves)]
    all_gather x1 -> x0, blocking collectives: 10.9 us -> none  [per_device(): gathered = lax.all_gather(paired, 'seq', axis=2, tiled=True)]
    ppermute x1, waiting for transfers between devices: 0.01 us -> 2.48 us  [swapped(): return lax.ppermute(block, axis, route)]
    all_gather x1, waiting for transfers between devices: 16.2 us -> 18.7 us  [joined(): everything = jax.tree.map(lambda part: lax.all_gather(part, axis), array)]
    unnamed x27 -> x39, local copies, waits for them, and re-layouts: 7.73 us -> 7 us
  transfers between devices with their start and end apart: 4 -> 11, of which waited for: 3 -> 10; matrix products, arithmetic and copies ran while one was open for 11% -> 10% of each run, Pallas kernels for 0% -> 0%
where the time goes in v1:
time: 188 us; the launch traced here: 187 us
  waiting for transfers between devices  68.6 us (36%)
  blocking collectives  53.7 us (29%)
  between operations  14.5 us (8%)
  matrix products  14.2 us (8%)
  local copies, waits for them, and re-layouts  13.7 us (7%)
  other arithmetic  13.2 us (7%)
  starting transfers between devices  7.8 us (4%)
    all_gather x2, blocking collectives, joined(): everything = jax.tree.map(lambda part: lax.all_gather(part, axis), array)  27.5 us
    ppermute x7, waiting for transfers between devices, close_the_plane(): item_now[dev] = jax.lax.ppermute(item_now[dev + 1], 'seq', leaves)  24.5 us
    all_gather x1, waiting for transfers between devices, joined(): everything = jax.tree.map(lambda part: lax.all_gather(part, axis), array)  18.7 us
    all_gather x1, waiting for transfers between devices, per_device(): lax.all_gather(out_weight, 'seq', axis=0, tiled=True)  15.3 us
    all_gather x1, blocking collectives, per_device(): queries = lax.all_gather(queries, ('grp', 'tp'), axis=0, tiled=True)  14.4 us
    psum x1, blocking collectives, per_device(): lax.psum((jnp.sum(query_raw * query_raw, axis=1), jnp.sum(key_raw * key_r...  11.8 us
    unnamed x39, local copies, waits for them, and re-layouts  7 us
    all_to_all x1, waiting for transfers between devices, per_device(): lax.all_to_all(attention, 'seq', split_axis=0, concat_axis=1, tiled=True)  6.99 us
  transfers between devices with their start and end apart: 11, of which 10 were waited for; matrix products, arithmetic and copies ran while one was open for 10% of the time, Pallas kernels for 0%

profile of v1, /device:TPU:0, one launch (start us, length us, event | category | flops | bytes accessed | tf_op | source)
XLA Modules:
  0.0 187.1 jit_solution(2520360465306774426)
XLA Ops:
  6.5 4.1 %collective-permute-start = (bf16[1,64,256]{2,1,0:T(8,128)(2,1)}, bf16[1,64,256]{2,1,0:T(8,128)(2,1)S(1)}, u32[]{:S(2)}, u32[]{:S(2)}) collective-permute-start(bf16[1,64,256]{2,1,0:T(8,128)(2,1)} %param.13), channel_id=1, source_target_pairs={{0,16},{16,0},{1,17},{17,1},{2,18},{18,2},{3,19},{19,3},{4,20},{20... | collective-permute-start | bytes 98312 | tf_op jit(solution)/shard_map/ppermute | solution.py:36
  10.6 2.5 %collective-permute-done = bf16[1,64,256]{2,1,0:T(8,128)(2,1)S(1)} collective-permute-done((bf16[1,64,256]{2,1,0:T(8,128)(2,1)}, bf16[1,64,256]{2,1,0:T(8,128)(2,1)S(1)}, u32[]{:S(2)}, u32[]{:S(2)}) %collective-permute-start) | collective-permute-done | bytes 32800 | tf_op jit(solution)/shard_map/ppermute | solution.py:36
  14.0 4.6 %collective-permute-done.1 = bf16[2,64,256]{2,1,0:T(8,128)(2,1)S(1)} collective-permute-done((bf16[2,64,256]{2,1,0:T(8,128)(2,1)S(1)}, bf16[2,64,256]{2,1,0:T(8,128)(2,1)S(1)}, u32[]{:S(2)}, u32[]{:S(2)}) %collective-permute-start.1) | collective-permute-done | bytes 65568 | tf_op jit(solution)/shard_map/ppermute | solution.py:18
  18.6 4.6 %collective-permute-done.2 = bf16[2,64,256]{2,1,0:T(8,128)(2,1)S(1)} collective-permute-done((bf16[2,64,256]{2,1,0:T(8,128)(2,1)S(1)}, bf16[2,64,256]{2,1,0:T(8,128)(2,1)S(1)}, u32[]{:S(2)}, u32[]{:S(2)}) %collective-permute-start.2) | collective-permute-done | bytes 65568 | tf_op jit(solution)/shard_map/ppermute | solution.py:18
  23.2 4.6 %collective-permute-done.3 = bf16[2,64,256]{2,1,0:T(8,128)(2,1)S(1)} collective-permute-done((bf16[2,64,256]{2,1,0:T(8,128)(2,1)S(1)}, bf16[2,64,256]{2,1,0:T(8,128)(2,1)S(1)}, u32[]{:S(2)}, u32[]{:S(2)}) %collective-permute-start.3) | collective-permute-done | bytes 65568 | tf_op jit(solution)/shard_map/ppermute | solution.py:18
  27.8 1.7 fusion.22
  29.5 2.9 %collective-permute-done.4 = bf16[2,64,256]{2,1,0:T(8,128)(2,1)S(1)} collective-permute-done((bf16[2,64,256]{2,1,0:T(8,128)(2,1)S(1)}, bf16[2,64,256]{2,1,0:T(8,128)(2,1)S(1)}, u32[]{:S(2)}, u32[]{:S(2)}) %collective-permute-start.4) | collective-permute-done | bytes 65568 | tf_op jit(solution)/shard_map/ppermute | solution.py:18
  33.7 6.3 %copy.28 = bf16[5120,3,128]{0,2,1:T(8,128)(2,1)} copy(bf16[5120,3,128]{2,0,1:T(8,128)(2,1)} %param.17) | data formatting | bytes 7864320 | tf_op args[4]
  42.1 3.3 %collective-permute-done.6 = bf16[2,64,256]{2,1,0:T(8,128)(2,1)S(1)} collective-permute-done((bf16[2,64,256]{2,1,0:T(8,128)(2,1)S(1)}, bf16[2,64,256]{2,1,0:T(8,128)(2,1)S(1)}, u32[]{:S(2)}, u32[]{:S(2)}) %collective-permute-start.6) | collective-permute-done | bytes 65568 | tf_op jit(solution)/shard_map/ppermute | solution.py:18
  45.4 4.6 %collective-permute-done.7 = bf16[2,64,256]{2,1,0:T(8,128)(2,1)S(1)} collective-permute-done((bf16[2,64,256]{2,1,0:T(8,128)(2,1)S(1)}, bf16[2,64,256]{2,1,0:T(8,128)(2,1)S(1)}, u32[]{:S(2)}, u32[]{:S(2)}) %collective-permute-start.7) | collective-permute-done | bytes 65568 | tf_op jit(solution)/shard_map/ppermute | solution.py:18
  50.3 1.7 fusion.9
  54.1 2.5 %fusion.11 = f32[512,256]{0,1:T(8,128)S(1)} fusion(f32[512,5120,1]{1,0,2:T(8,128)S(1)} %get-tuple-element.357, f32[5120]{0:T(1024)S(1)} %bitcast.97, f32[5120]{0:T(1024)S(1)} %bitcast.95, f32[512]{0:T(512)S(1)} %add_rsqrt_fusion.1, f32[512]{0:T(512)S(1)} %broadcast_multiply_fusion, f32[5120]{0:T(1024)S(1)} %copy-done.2, bf16[5120,384]{0,1:T(8,128)(2,1)S(1)} %bitcast.83), kind=kOutput, calls=%fused_computation.26 | convolution fusion | flops 1357905920 | bytes 13697024 | tf_op jit(solution)/shard_map/while/body/eval_jaxpr/dot_general | solution.py:71
  61.8 2.6 %multiply_reduce_fusion.3 = (f32[256]{0:T(256)S(1)}, f32[256,128]{0,1:T(8,128)S(1)}) fusion(bf16[5120,384]{0,1:T(8,128)(2,1)} %bitcast.82, f32[256,5120]{1,0:T(8,128)S(1)} %get-tuple-element.353, f32[5120]{0:T(1024)S(1)} %bitcast.98, f32[5120]{0:T(1024)S(1)} %bitcast.96, f32[256]{0:T(256)S(1)} %add_rsqrt_fusion.3, f32[256]{0:T(256)S(1)} %broadcast_multiply_fusion.1), kind=kOutput, calls=%fused_computation.42 | convolution fusion | flops 342163200 | bytes 6728704 | tf_op jit(solution)/shard_map/while/body/eval_jaxpr/dot_general | solution.py:71
  64.4 11.8 %all-reduce = (f32[256]{0:T(256)S(1)}, f32[512]{0:T(512)S(1)}) all-reduce(f32[256]{0:T(256)S(1)} %get-tuple-element.354, f32[512]{0:T(512)S(1)} %multiply_reduce_fusion.2), channel_id=1, replica_groups=mesh['grp'=2,'seq'=8,'tp'=2] {'seq'}, use_global_device_ids=true, to_apply=%region_3.4 | all-reduce | flops 768 | bytes 6144 | tf_op jit(solution)/shard_map/psum | solution.py:115
  76.5 14.4 %all_gather.15 = bf16[1024,128]{0,1:T(8,128)(2,1)S(1)} all-gather(bf16[256,128]{0,1:T(8,128)(2,1)S(1)} %multiply_convert_fusion.1), channel_id=1, replica_groups=mesh['grp'=2,'seq'=8,'tp'=2] {'grp','tp'}, dimensions={0}, use_global_device_ids=true | all-gather | bytes 327680 | tf_op jit(solution)/shard_map/all_gather | solution.py:125
  91.1 5.8 %while.11 = (s32[]{:T(128)}, f32[2,512]{1,0:T(2,128)S(1)}, f32[2,512]{1,0:T(2,128)S(1)}, f32[2,512,128]{2,1,0:T(8,128)}, s32[2]{0:T(128)S(1)}, /*index=5*/bf16[1...) while((s32[]{:T(128)}, f32[2,512]{1,0:T(2,128)S(1)}, ...), condition=%wide.region_11.12_spmd, body=%wide.region_8.11_spmd.sunk | while | flops 135789568 | bytes 3818171 | solution.py:144
  97.6 13.6 %all-gather = f32[4,1,1024]{2,1,0:T(1,128)S(1)} all-gather(f32[1,1,1024]{2,1,0:T(1,128)S(1)} %reshape.73), channel_id=1, replica_groups=mesh['grp'=2,'seq'=8,'tp'=2] {'grp','tp'}, dimensions={0}, use_global_device_ids=true | all-gather | bytes 20480 | tf_op jit(solution)/shard_map/all_gather | solution.py:40
  111.2 13.9 %all-gather.1 = f32[4,1,1024]{2,1,0:T(1,128)S(1)} all-gather(f32[1,1,1024]{2,1,0:T(1,128)S(1)} %reshape.75), channel_id=1, replica_groups=mesh['grp'=2,'seq'=8,'tp'=2] {'grp','tp'}, dimensions={0}, use_global_device_ids=true | all-gather | bytes 20480 | tf_op jit(solution)/shard_map/all_gather | solution.py:40
  125.1 18.7 %all-gather.5.cloned.1.call-done = f32[4,1024,128]{2,1,0:T(8,128)} async-done(((f32[1,1024,128]{2,1,0:T(8,128)}), f32[4,1024,128]{2,1,0:T(8,128)}) %all-gather.5.cloned.1.call-update) | async-done | bytes 2097168 | tf_op jit(solution)/shard_map/all_gather | solution.py:40
  144.9 4.7 %while.42 = (s32[]{:T(128)}, f32[1024]{0:T(1024)S(1)}, f32[1024]{0:T(1024)S(1)}, f32[1024,128]{1,0:T(8,128)S(1)}, f32[4,1024]{1,0:T(4,128)S(1)}, /*index=5*/f32[...) while((s32[]{:T(128)}, f32[1024]{0:T(1024)S(1)}, f32[1024]{0:T(1024)S(1)}, ...), condition=%wide.region_13.14_spmd, body=%wide.region_12.13_spmd.sunk | while | flops 399365 | bytes 1630359 | solution.py:46
  150.5 3.6 %all-to-all-start = ((bf16[8,128,128]{2,1,0:T(8,128)(2,1)}), bf16[8,128,128]{2,1,0:T(8,128)(2,1)S(1)}, u32[]{:S(2)}, u32[]{:S(2)}) async-start(bf16[8,128,128]{2,1,0:T(8,128)(2,1)} %bitcast.21), calls=%async_computation | async-start | bytes 524288 | tf_op jit(solution)/shard_map/all_to_all | solution.py:161
  154.8 7.0 %all-to-all-done = bf16[8,128,128]{2,1,0:T(8,128)(2,1)S(1)} async-done(((bf16[8,128,128]{2,1,0:T(8,128)(2,1)}), bf16[8,128,128]{2,1,0:T(8,128)(2,1)S(1)}, u32[]{:S(2)}, u32[]{:S(2)}) %all-to-all-start) | async-done | bytes 262176 | tf_op jit(solution)/shard_map/all_to_all | solution.py:161
  161.9 15.3 %all-gather.7.cloned.1.call-done = bf16[1024,1280]{1,0:T(8,128)(2,1)} async-done(((bf16[128,1280]{1,0:T(8,128)(2,1)}), bf16[1024,1280]{1,0:T(8,128)(2,1)}) %all-gather.7.cloned.1.call-update) | async-done | bytes 2621456 | tf_op jit(solution)/shard_map/all_gather | solution.py:164
  177.2 3.0 %fusion.14 = bf16[128,1280]{1,0:T(8,128)(2,1)} fusion(bf16[128,1024]{0,1:T(8,128)(2,1)S(1)} %bitcast.84, bf16[1024,1280]{1,0:T(8,128)(2,1)} %all-gather.7.cloned.1.call-done, f32[1280]{0:T(1024)S(1)} %dynamic-slice_reduce_fusion), kind=kOutput, calls=%fused_computation.30 | convolution fusion | flops 335872000 | bytes 3216384 | tf_op jit(solution)/shard_map/dot_general | solution.py:162
  (106 shorter events, 24.1 us)
Async XLA Ops:
  6.5 43.7 %copy-start = (bf16[128,5120]{1,0:T(8,128)(2,1)S(1)}, bf16[128,5120]{1,0:T(8,128)(2,1)}, u32[]{:S(2)}) copy-start(bf16[128,5120]{1,0:T(8,128)(2,1)} %param.14) | copy-start | bytes 3932164
  6.5 43.5 %copy-start.3 = (bf16[1,64,256]{2,1,0:T(8,128)(2,1)S(1)}, bf16[1,64,256]{2,1,0:T(8,128)(2,1)}, u32[]{:S(2)}) copy-start(bf16[1,64,256]{2,1,0:T(8,128)(2,1)} %param.13) | copy-start | bytes 98308
  6.5 137.3 %all-gather.5.cloned.1.call-start = ((), (), s32[]{:S(2)}) async-start(), calls=%async_computation.1 | async-start | bytes 2621440 | tf_op jit(solution)/shard_map/all_gather | solution.py:40
  6.5 6.5 %collective-permute-start = (bf16[1,64,256]{2,1,0:T(8,128)(2,1)}, bf16[1,64,256]{2,1,0:T(8,128)(2,1)S(1)}, u32[]{:S(2)}, u32[]{:S(2)}) collective-permute-start(bf16[1,64,256]{2,1,0:T(8,128)(2,1)} %param.13), channel_id=1, source_target_pairs={{0,16},{16,0},{1,17},{17,1},{2,18},{18,2},{3,19},{19,3},{4,20},{20... | collective-permute-start | bytes 98312 | tf_op jit(solution)/shard_map/ppermute | solution.py:36
  13.9 4.6 %collective-permute-start.1 = (bf16[2,64,256]{2,1,0:T(8,128)(2,1)S(1)}, bf16[2,64,256]{2,1,0:T(8,128)(2,1)S(1)}, u32[]{:S(2)}, u32[]{:S(2)}) collective-permute-start(bf16[2,64,256]{2,1,0:T(8,128)(2,1)S(1)} %maximum_select_fusion), channel_id=1, source_target_pairs={{0,2},{2,4},{4,6},{6,8},{8,10},{10,12},{12,14},{14,0},{1,3},{3,5},... | collective-permute-start | bytes 196616 | tf_op jit(solution)/shard_map/ppermute | solution.py:18
  18.6 4.6 %collective-permute-start.2 = (bf16[2,64,256]{2,1,0:T(8,128)(2,1)S(1)}, bf16[2,64,256]{2,1,0:T(8,128)(2,1)S(1)}, u32[]{:S(2)}, u32[]{:S(2)}) collective-permute-start(bf16[2,64,256]{2,1,0:T(8,128)(2,1)S(1)} %collective-permute-done.1), channel_id=1, source_target_pairs={{0,2},{2,4},{4,6},{6,8},{8,10},{10,12},{12,14},{14,0},{1,3},{3,5},... | collective-permute-start | bytes 196616 | tf_op jit(solution)/shard_map/ppermute | solution.py:18
  23.2 4.6 %collective-permute-start.3 = (bf16[2,64,256]{2,1,0:T(8,128)(2,1)S(1)}, bf16[2,64,256]{2,1,0:T(8,128)(2,1)S(1)}, u32[]{:S(2)}, u32[]{:S(2)}) collective-permute-start(bf16[2,64,256]{2,1,0:T(8,128)(2,1)S(1)} %collective-permute-done.2), channel_id=1, source_target_pairs={{0,2},{2,4},{4,6},{6,8},{8,10},{10,12},{12,14},{14,0},{1,3},{3,5},... | collective-permute-start | bytes 196616 | tf_op jit(solution)/shard_map/ppermute | solution.py:18
  27.8 4.6 %collective-permute-start.4 = (bf16[2,64,256]{2,1,0:T(8,128)(2,1)S(1)}, bf16[2,64,256]{2,1,0:T(8,128)(2,1)S(1)}, u32[]{:S(2)}, u32[]{:S(2)}) collective-permute-start(bf16[2,64,256]{2,1,0:T(8,128)(2,1)S(1)} %collective-permute-done.3), channel_id=1, source_target_pairs={{0,2},{2,4},{4,6},{6,8},{8,10},{10,12},{12,14},{14,0},{1,3},{3,5},... | collective-permute-start | bytes 196616 | tf_op jit(solution)/shard_map/ppermute | solution.py:18
  29.5 24.1 %copy-start.4 = (f32[1,5120]{1,0:T(1,128)}, f32[1,5120]{1,0:T(1,128)S(1)}, u32[]{:S(2)}) copy-start(f32[1,5120]{1,0:T(1,128)S(1)} %get-tuple-element.348) | copy-start | bytes 61444
  29.5 24.1 %copy-start.6 = (f32[1,5120]{1,0:T(1,128)}, f32[1,5120]{1,0:T(1,128)S(1)}, u32[]{:S(2)}) copy-start(f32[1,5120]{1,0:T(1,128)S(1)} %get-tuple-element.349) | copy-start | bytes 61444
  32.4 8.4 %collective-permute-start.5 = (bf16[2,64,256]{2,1,0:T(8,128)(2,1)S(1)}, bf16[2,64,256]{2,1,0:T(8,128)(2,1)S(1)}, u32[]{:S(2)}, u32[]{:S(2)}) collective-permute-start(bf16[2,64,256]{2,1,0:T(8,128)(2,1)S(1)} %collective-permute-done.4), channel_id=1, source_target_pairs={{0,2},{2,4},{4,6},{6,8},{8,10},{10,12},{12,14},{14,0},{1,3},{3,5},... | collective-permute-start | bytes 196616 | tf_op jit(solution)/shard_map/ppermute | solution.py:18
  33.7 16.6 %copy-start.2 = (f32[5120]{0:T(1024)S(1)}, f32[5120]{0:T(1024)}, u32[]{:S(2)}) copy-start(f32[5120]{0:T(1024)} %param.15) | copy-start | bytes 61444
  40.7 4.6 %collective-permute-start.6 = (bf16[2,64,256]{2,1,0:T(8,128)(2,1)S(1)}, bf16[2,64,256]{2,1,0:T(8,128)(2,1)S(1)}, u32[]{:S(2)}, u32[]{:S(2)}) collective-permute-start(bf16[2,64,256]{2,1,0:T(8,128)(2,1)S(1)} %collective-permute-done.5), channel_id=1, source_target_pairs={{0,2},{2,4},{4,6},{6,8},{8,10},{10,12},{12,14},{14,0},{1,3},{3,5},... | collective-permute-start | bytes 196616 | tf_op jit(solution)/shard_map/ppermute | solution.py:18
  45.4 4.6 %collective-permute-start.7 = (bf16[2,64,256]{2,1,0:T(8,128)(2,1)S(1)}, bf16[2,64,256]{2,1,0:T(8,128)(2,1)S(1)}, u32[]{:S(2)}, u32[]{:S(2)}) collective-permute-start(bf16[2,64,256]{2,1,0:T(8,128)(2,1)S(1)} %collective-permute-done.6), channel_id=1, source_target_pairs={{0,2},{2,4},{4,6},{6,8},{8,10},{10,12},{12,14},{14,0},{1,3},{3,5},... | collective-permute-start | bytes 196616 | tf_op jit(solution)/shard_map/ppermute | solution.py:18
  52.0 2.1 %copy-start.1 = (bf16[5120,3,128]{0,2,1:T(8,128)(2,1)S(1)}, bf16[5120,3,128]{0,2,1:T(8,128)(2,1)}, u32[]{:S(2)}) copy-start(bf16[5120,3,128]{0,2,1:T(8,128)(2,1)} %copy.28) | copy-start | bytes 11796484
  59.4 2.4 %copy-start.5 = (f32[1,5120]{1,0:T(1,128)S(1)}, f32[1,5120]{1,0:T(1,128)}, u32[]{:S(2)}) copy-start(f32[1,5120]{1,0:T(1,128)} %copy-done.4) | copy-start | bytes 61444
  59.4 2.4 %copy-start.7 = (f32[1,5120]{1,0:T(1,128)S(1)}, f32[1,5120]{1,0:T(1,128)}, u32[]{:S(2)}) copy-start(f32[1,5120]{1,0:T(1,128)} %copy-done.6) | copy-start | bytes 61444
  61.8 14.4 %copy-start.9 = (f32[128]{0:T(128)S(1)}, f32[128]{0:T(128)}, u32[]{:S(2)}) copy-start(f32[128]{0:T(128)} %get-tuple-element.350) | copy-start | bytes 1540
  61.8 14.6 %copy-start.8 = (f32[128]{0:T(128)S(1)}, f32[128]{0:T(128)}, u32[]{:S(2)}) copy-start(f32[128]{0:T(128)} %get-tuple-element.351) | copy-start | bytes 1540
  96.9 80.4 %all-gather.7.cloned.1.call-start = ((), (), s32[]{:S(2)}) async-start(), calls=%async_computation.2 | async-start | bytes 2949120 | tf_op jit(solution)/shard_map/all_gather | solution.py:164
  150.5 11.3 %all-to-all-start = ((bf16[8,128,128]{2,1,0:T(8,128)(2,1)}), bf16[8,128,128]{2,1,0:T(8,128)(2,1)S(1)}, u32[]{:S(2)}, u32[]{:S(2)}) async-start(bf16[8,128,128]{2,1,0:T(8,128)(2,1)} %bitcast.21), calls=%async_computation | async-start | bytes 524288 | tf_op jit(solution)/shard_map/all_to_all | solution.py:161
Sparse Core Ops, SparseCore 0:
  97.0 46.7 all-gather.4
  145.7 31.4 all-gather.6
